TPU v7x, 32 devices: a whole 2x2x4 slice. The times are simulated.
32 devices in a mesh: groups: 2 (over x), mp: 4 (over y, core), dp: 4 (over z).
Axes of the slice: x: 2, y: 2, z: 4, core: 2. Of those that a mesh axis runs over, the one named last changes fastest.
Arguments:
- grid_feat: bfloat16 [8, 512, 1024], P(('groups', 'dp'), 'mp'), parts along dimension 0, may hold values from -6 to 6
- node_feat: bfloat16 [8, 256, 1024], P(('groups', 'dp'), 'mp'), parts along dimension 0, may hold values from -6 to 6
- cotangent: bfloat16 [8, 512, 1024], P(('groups', 'dp'), 'mp'), parts along dimension 0, may hold values from -6 to 6
- w_query: bfloat16 [1024, 1024], replicated, may hold values from -2 to 2, as said below
- w_keyval: bfloat16 [1024, 2048], replicated, may hold values from -2 to 2, as said below
- neighbours: int32 [512, 12], P('mp'), may hold values from 0 to 127, as said below
- send_rows: int32 [4, 4, 16], P('mp'), may hold values from 0 to 63, as said below
Outputs:
- d_grid: bfloat16 [8, 512, 1024], P(('groups', 'dp'), 'mp'), parts along dimension 0
- d_nodes: bfloat16 [8, 256, 1024], P(('groups', 'dp'), 'mp'), parts along dimension 0
- dw_query: float32 [2048, 1024], P(('groups', 'mp', 'dp')), parts along dimension 0
- dw_keyval: float32 [2048, 2048], P(('groups', 'mp', 'dp')), parts along dimension 0
There are 2 independent parts, one for each index of `groups`. A program takes and returns all parts, laid end to end along the dimension named above; an argument that names none is the same for every part. Nothing has to cross between parts.
Inputs may be any that keep to these rules, and one draw needn't show every extreme that they name: `neighbours`: an entry under 4 * 16 names slot r % 16 of the block that index r // 16 of mp sends to the grid point's own index; larger entries name the own index's nodes. The slots that are named in a block form a leading run; every index names all 16 slots of the blocks from the indices one below and one above it on mp (wrapping around), some of every other index's block, and none of its own block. `send_rows`: the 16 rows of one block are distinct local node rows of the sending index. `w_query`: projection weights. `w_keyval`: projection weights.
All inputs are finite; a program needn't handle non-finite values.
Results may differ from a plain program's by a relative error of at most 0.018.
The roundings to bfloat16 on the way count: a program that leaves them out, or rounds other values in their place, can miss the bound.
Values may be sent and summed in bfloat16 or wider, within the bound.
A program may use at most 128 MiB of HBM per device.

v0:
```python
import math

import jax
import jax.numpy as jnp
from jax import lax
from jax.sharding import PartitionSpec as P

HEADS = 16


HIGH = lax.Precision.HIGHEST


def block_grads(query_rows, cot_rows, ids, table):
    count, width = query_rows.shape
    nbrs = ids.shape[1]
    total_rows = table.shape[0]
    scale = (width // HEADS) ** (-0.5)
    edges = table[ids]
    keys_bf = edges[:, :, :width].reshape(count, nbrs, HEADS, -1)
    values_bf = edges[:, :, width:].reshape(count, nbrs, HEADS, -1)
    query_bf = query_rows.reshape(count, HEADS, -1)
    cot_bf = cot_rows.reshape(count, HEADS, -1)
    scores = (
        jnp.einsum("ghe,gkhe->gkh", query_bf, keys_bf, preferred_element_type=jnp.float32) * scale
    )
    attn = jax.nn.softmax(scores, axis=1)
    d_attn = jnp.einsum("ghe,gkhe->gkh", cot_bf, values_bf, preferred_element_type=jnp.float32)
    d_scores = attn * (d_attn - jnp.sum(attn * d_attn, axis=1, keepdims=True))
    keys_full = keys_bf.astype(jnp.float32)
    d_query = (
        (jnp.einsum("gkh,gkhe->ghe", d_scores, keys_full, precision=HIGH) * scale)
        .reshape(count, width)
        .astype(jnp.bfloat16)
    )
    onehot = (ids[:, :, None] == jnp.arange(total_rows, dtype=jnp.int32)[None, None, :]).astype(
        jnp.float32
    )
    key_weight = jnp.einsum("gkr,gkh->hrg", onehot, d_scores * scale, precision=HIGH)
    value_weight = jnp.einsum("gkr,gkh->hrg", onehot, attn, precision=HIGH)
    d_keys = jnp.einsum(
        "hrg,ghe->rhe", key_weight, query_bf.astype(jnp.float32), precision=HIGH
    ).reshape(total_rows, width)
    d_values = jnp.einsum(
        "hrg,ghe->rhe", value_weight, cot_bf.astype(jnp.float32), precision=HIGH
    ).reshape(total_rows, width)
    return (d_query, d_keys, d_values)


def per_device(grid_feat, node_feat, cotangent, w_query, w_keyval, neighbours, send_rows):
    count_mp = lax.axis_size("mp")
    count_dp = lax.axis_size("dp")
    samples_dev, grid_dev, width = grid_feat.shape
    nodes_dev = node_feat.shape[1]
    slots = send_rows.shape[1] * send_rows.shape[2]
    outgoing_rows = send_rows[0].reshape(-1)
    block = min(128, grid_dev)
    blocks = grid_dev // block
    wscale = 1.0 / math.sqrt(samples_dev * count_dp * grid_dev * count_mp)
    dims_t = (((0,), (0,)), ((), ()))
    dims_w = (((1,), (1,)), ((), ()))
    grid_x = grid_feat[0]
    node_x = node_feat[0]
    query = jnp.dot(grid_x, w_query, preferred_element_type=jnp.float32).astype(jnp.bfloat16)
    keyval = jnp.dot(node_x, w_keyval, preferred_element_type=jnp.float32).astype(jnp.bfloat16)
    outgoing = keyval[outgoing_rows].reshape(count_mp, -1, 2 * width)
    arrived = lax.all_to_all(outgoing, "mp", split_axis=0, concat_axis=0, tiled=True)
    table = jnp.concatenate([arrived.reshape(slots, 2 * width), keyval], axis=0)

    def block_step(buffers, pieces):
        query_rows, cot_rows, ids = pieces
        d_query, d_keys, d_values = block_grads(query_rows, cot_rows, ids, table)
        return ((buffers[0] + d_keys, buffers[1] + d_values), d_query)

    empty = jnp.zeros((slots + nodes_dev, width), jnp.float32)
    pieces = (
        query.reshape(blocks, block, width),
        cotangent[0].reshape(blocks, block, width),
        neighbours.reshape(blocks, block, -1),
    )
    (key_sum, value_sum), d_query = lax.scan(block_step, (empty, empty), pieces)
    d_query = d_query.reshape(grid_dev, width)
    partial_value = jnp.concatenate([key_sum, value_sum], axis=1).astype(jnp.bfloat16)
    returned = lax.all_to_all(
        partial_value[:slots].reshape(count_mp, -1, 2 * width),
        "mp",
        split_axis=0,
        concat_axis=0,
        tiled=True,
    )
    own = lax.optimization_barrier(partial_value[slots:]).astype(jnp.float32)
    dkv = (
        own.at[outgoing_rows]
        .add(returned.reshape(slots, 2 * width).astype(jnp.float32))
        .astype(jnp.bfloat16)
    )
    grid_out = [
        lax.dot_general(d_query, w_query, dims_w, preferred_element_type=jnp.float32).astype(
            jnp.bfloat16
        )
    ]
    node_out = [
        lax.dot_general(dkv, w_keyval, dims_w, preferred_element_type=jnp.float32).astype(
            jnp.bfloat16
        )
    ]
    term_q = lax.dot_general(grid_x, d_query, dims_t, preferred_element_type=jnp.float32) * wscale
    term_kv = lax.dot_general(node_x, dkv, dims_t, preferred_element_type=jnp.float32) * wscale
    model_q, model_kv = (
        lax.psum_scatter(term_q.astype(jnp.bfloat16), "mp", scatter_dimension=0, tiled=True).astype(
            jnp.float32
        ),
        lax.psum_scatter(
            term_kv.astype(jnp.bfloat16), "mp", scatter_dimension=0, tiled=True
        ).astype(jnp.float32),
    )
    total_q, total_kv = (
        lax.psum_scatter(
            model_q.astype(jnp.bfloat16), "dp", scatter_dimension=0, tiled=True
        ).astype(jnp.float32),
        lax.psum_scatter(
            model_kv.astype(jnp.bfloat16), "dp", scatter_dimension=0, tiled=True
        ).astype(jnp.float32),
    )
    return (jnp.stack(grid_out), jnp.stack(node_out), total_q, total_kv)


def solution(mesh):
    in_specs = (
        P(("groups", "dp"), "mp", None),
        P(("groups", "dp"), "mp", None),
        P(("groups", "dp"), "mp", None),
        P(),
        P(),
        P("mp", None),
        P("mp", None, None),
    )
    out_specs = (
        P(("groups", "dp"), "mp", None),
        P(("groups", "dp"), "mp", None),
        P(("groups", "mp", "dp"), None),
        P(("groups", "mp", "dp"), None),
    )
    return jax.shard_map(
        per_device, mesh=mesh, in_specs=in_specs, out_specs=out_specs, check_vma=False
    )
```

profile of v0, /device:TPU:0, one launch (start us, length us, event | category | flops | bytes accessed | tf_op | source)
XLA Modules:
  0.0 226.7 jit_solution(9846673428729864841)
XLA Ops:
  8.1 3.1 %convolution_convert_fusion = bf16[64,2048]{1,0:T(8,128)(2,1)S(1)} fusion(bf16[1024,2048]{1,0:T(8,128)(2,1)} %param.11, bf16[1,64,1024]{2,1,0:T(8,128)(2,1)} %param.8), kind=kOutput, calls=%fused_computation.9 | convolution fusion | flops 268566528 | bytes 4587520 | tf_op jit(solution)/shard_map/dot_general | solution.py:65
  12.7 4.3 %all-to-all-start = ((bf16[4,16,2048]{2,1,0:T(8,128)(2,1)}), bf16[4,16,2048]{2,1,0:T(8,128)(2,1)}, u32[]{:S(2)}, u32[]{:S(2)}) async-start(bf16[4,16,2048]{2,1,0:T(8,128)(2,1)} %bitcast.6), calls=%async_computation | async-start | bytes 524288 | tf_op jit(solution)/shard_map/all_to_all | solution.py:67
  19.0 4.5 %all-to-all-done = bf16[4,16,2048]{2,1,0:T(8,128)(2,1)} async-done(((bf16[4,16,2048]{2,1,0:T(8,128)(2,1)}), bf16[4,16,2048]{2,1,0:T(8,128)(2,1)}, u32[]{:S(2)}, u32[]{:S(2)}) %all-to-all-start) | async-done | bytes 262176 | tf_op jit(solution)/shard_map/all_to_all | solution.py:67
  24.5 7.1 %gather_fusion.1 = bf16[1536,2048]{1,0:T(8,128)(2,1)} fusion(bf16[128,2048]{1,0:T(8,128)(2,1)S(1)} %pad_maximum_fusion, s32[2048]{0:T(1024)S(1)} %pad_clamp_fusion), kind=kCustom, calls=%fused_computation.1 | custom fusion | bytes 12589056 | tf_op jit(solution)/shard_map/while/body/eval_jaxpr/gather | solution.py:19
  31.6 10.6 %reshape.111 = bf16[128,12,2048]{2,1,0:T(8,128)(2,1)} reshape(bf16[1536,2048]{1,0:T(8,128)(2,1)} %gather_fusion.1) | data formatting | bytes 12582912 | tf_op jit(solution)/shard_map/while/body/eval_jaxpr/gather | solution.py:19
  42.2 6.3 %fusion.30 = (bf16[128,12,1024]{2,1,0:T(8,128)(2,1)}, bf16[128,12,1024]{2,1,0:T(8,128)(2,1)}) fusion(bf16[128,12,2048]{2,1,0:T(8,128)(2,1)} %reshape.111), kind=kLoop, calls=%fused_computation.58 | loop fusion | bytes 12582912 | tf_op jit(solution)/shard_map/while/body/eval_jaxpr/slice | solution.py:21
  48.5 6.4 %copy.59 = bf16[128,12,1024]{0,2,1:T(8,128)(2,1)} copy(bf16[128,12,1024]{2,1,0:T(8,128)(2,1)} %get-tuple-element.41) | data formatting | bytes 6291456
  54.8 3.0 %multiply_reduce_fusion.2 = f32[128,16,12]{0,1,2:T(8,128)S(1)} fusion(f32[128,16,64]{0,2,1:T(8,128)S(1)} %bitcast_convert_fusion, bf16[128,12,1024]{0,2,1:T(8,128)(2,1)} %copy.59), kind=kLoop, calls=%fused_computation.6 | loop fusion | flops 4694016 | bytes 3768320
  59.4 6.4 %copy.60 = bf16[128,12,1024]{0,2,1:T(8,128)(2,1)} copy(bf16[128,12,1024]{2,1,0:T(8,128)(2,1)} %get-tuple-element.40) | data formatting | bytes 6291456
  65.7 3.2 %multiply_reduce_fusion.1 = f32[128,16,12]{0,1,2:T(8,128)S(1)} fusion(f32[128,16,64]{0,2,1:T(8,128)} %convert.16, bf16[128,12,1024]{0,2,1:T(8,128)(2,1)} %copy.60), kind=kLoop, calls=%fused_computation.5 | loop fusion | flops 4694016 | bytes 3768320
  70.4 2.0 fusion.4
  73.1 2.8 %fusion.18 = f32[128,16,12]{2,1,0:T(8,128)} fusion(f32[128,16]{1,0:T(8,128)S(1)} %fusion.4, f32[128,16,12]{2,1,0:T(8,128)} %copy.51, f32[128,16]{1,0:T(8,128)S(1)} %fusion.11, f32[128,16]{1,0:T(8,128)S(1)} %bitcast_reduce_fusion, f32[128,16,12]{2,1,0:T(8,128)S(1)} %copy.44), kind=kLoop, calls=%fused_computation.42 | loop fusion | flops 122880 | bytes 319488
  75.9 1.6 copy.68
  77.5 2.7 %multiply_reduce_fusion = f32[128,16,64]{0,2,1:T(8,128)S(1)} fusion(bf16[128,16,12,64]{0,3,1,2:T(8,128)(2,1)} %bitcast.93, f32[128,16,12]{0,1,2:T(8,128)S(1)} %copy.68), kind=kLoop, calls=%fused_computation.4 | loop fusion | flops 4587520 | bytes 3768320 | tf_op jit(solution)/shard_map/while/body/eval_jaxpr/gkh,gkhe->ghe/dot_general | solution.py:32
  80.3 3.0 %fusion.1 = bf16[1024,1024]{0,1:T(8,128)(2,1)} fusion(bf16[128,1024]{0,1:T(8,128)(2,1)S(1)} %bitcast.94, bf16[1,128,1024]{2,1,0:T(8,128)(2,1)} %param.7), kind=kOutput, calls=%fused_computation.10 | convolution fusion | flops 270532608 | bytes 2621440 | tf_op jit(solution)/shard_map/dot_general | solution.py:107
  84.1 3.7 %convolution_bitcast_fusion.1 = f32[16,128,128]{1,0,2:T(8,128)S(1)} fusion(s32[128,12]{1,0:T(8,128)} %copy.31, f32[128,16,12]{2,1,0:T(8,128)} %copy.51, f32[128,16]{1,0:T(8,128)} %copy-done.7, f32[128,16,12]{2,1,0:T(8,128)S(1)} %copy.44, f32[128,16]{1,0:T(8,128)S(1)} %fusion.11, f32[128,16]{1,0:T(8,128)S(1)} %bitcast_reduce_fusion), kind=kOutput, calls=%fused_computation.12 | convolution fusion | flops 38092800 | bytes 1275904 | tf_op jit(solution)/shard_map/while/body/eval_jaxpr/gkr,gkh->hrg/dot_general | solution.py:39
  87.8 1.6 convolution_convert_fusion.2
  89.4 1.8 copy.34
  91.2 3.1 %convolution_bitcast_fusion = f32[16,128,128]{1,0,2:T(8,128)S(1)} fusion(s32[128,12]{1,0:T(8,128)} %copy.31, f32[128,16,12]{2,1,0:T(8,128)S(1)} %copy.44, f32[128,16]{1,0:T(8,128)S(1)} %fusion.11, f32[128,16]{1,0:T(8,128)S(1)} %bitcast_reduce_fusion), kind=kOutput, calls=%fused_computation.11 | convolution fusion | flops 38019072 | bytes 1169408 | tf_op jit(solution)/shard_map/while/body/eval_jaxpr/gkr,gkh->hrg/dot_general | solution.py:40
  95.4 1.7 pad_maximum_fusion.1
  97.1 3.4 %all-to-all-start.1 = ((bf16[4,16,2048]{2,1,0:T(8,128)(2,1)}), bf16[4,16,2048]{2,1,0:T(8,128)(2,1)S(1)}, u32[]{:S(2)}, u32[]{:S(2)}) async-start(bf16[4,16,2048]{2,1,0:T(8,128)(2,1)} %bitcast.29), calls=%async_computation.1 | async-start | bytes 524288 | tf_op jit(solution)/shard_map/all_to_all | solution.py:84
  100.6 8.9 %all-to-all-done.1 = bf16[4,16,2048]{2,1,0:T(8,128)(2,1)S(1)} async-done(((bf16[4,16,2048]{2,1,0:T(8,128)(2,1)}), bf16[4,16,2048]{2,1,0:T(8,128)(2,1)S(1)}, u32[]{:S(2)}, u32[]{:S(2)}) %all-to-all-start.1) | async-done | bytes 262176 | tf_op jit(solution)/shard_map/all_to_all | solution.py:84
  109.5 1.6 scatter_custom_fusion
  111.2 3.2 %fusion = bf16[1024,2048]{0,1:T(8,128)(2,1)} fusion(bf16[1,64,1024]{2,1,0:T(8,128)(2,1)S(1)} %copy-done.6, f32[64,2048]{1,0:T(8,128)S(1)} %scatter_custom_fusion), kind=kOutput, calls=%fused_computation.8 | convolution fusion | flops 272760832 | bytes 4849664 | tf_op jit(solution)/shard_map/dot_general | solution.py:108
  114.4 4.1 %reduce-scatter.9.cloned.1.call-done = bf16[256,1024]{0,1:T(8,128)(2,1)} async-done(((bf16[1024,1024]{0,1:T(8,128)(2,1)}), bf16[256,1024]{0,1:T(8,128)(2,1)}) %reduce-scatter.9.cloned.1.call-update) | async-done | bytes 524304 | tf_op jit(solution)/shard_map/reduce_scatter | solution.py:110
  118.5 2.0 copy.62
  120.7 44.8 %reduce-scatter.11.cloned.1.call-done = bf16[256,2048]{0,1:T(8,128)(2,1)} async-done(((bf16[1024,2048]{0,1:T(8,128)(2,1)}), bf16[256,2048]{0,1:T(8,128)(2,1)}) %reduce-scatter.11.cloned.1.call-update) | async-done | bytes 1048592 | tf_op jit(solution)/shard_map/reduce_scatter | solution.py:113
  165.5 2.3 %copy.64 = bf16[256,2048]{1,0:T(8,128)(2,1)} copy(bf16[256,2048]{0,1:T(8,128)(2,1)} %reduce-scatter.11.cloned.1.call-done) | data formatting | bytes 2097152
  167.8 1.5 fusion.2
  169.3 4.2 %fusion.3 = bf16[1,64,1024]{2,1,0:T(8,128)(2,1)} fusion(bf16[1024,2048]{1,0:T(8,128)(2,1)} %param.11, f32[64,2048]{1,0:T(8,128)S(1)} %scatter_custom_fusion), kind=kOutput, calls=%fused_computation.19 | convolution fusion | flops 268632064 | bytes 4849664 | tf_op jit(solution)/shard_map/dot_general | solution.py:103
  173.6 16.7 %reduce-scatter.13.cloned.1.call-done = bf16[64,1024]{1,0:T(8,128)(2,1)} async-done(((bf16[256,1024]{1,0:T(8,128)(2,1)}), bf16[64,1024]{1,0:T(8,128)(2,1)}) %reduce-scatter.13.cloned.1.call-update) | async-done | bytes 131088
  192.1 25.8 %reduce-scatter.15.cloned.1.call-done = bf16[64,2048]{1,0:T(8,128)(2,1)} async-done(((bf16[256,2048]{1,0:T(8,128)(2,1)}), bf16[64,2048]{1,0:T(8,128)(2,1)}) %reduce-scatter.15.cloned.1.call-update) | async-done | bytes 262160
  (55 shorter events, 15.1 us)
Async XLA Ops:
  7.2 10.1 %copy-start = (bf16[1024,1024]{1,0:T(8,128)(2,1)S(1)}, bf16[1024,1024]{1,0:T(8,128)(2,1)}, u32[]{:S(2)}) copy-start(bf16[1024,1024]{1,0:T(8,128)(2,1)} %param.10) | copy-start | bytes 6291460
  7.2 9.8 %copy-start.9 = (s32[128,12]{0,1:T(8,128)S(1)}, s32[128,12]{0,1:T(8,128)}, u32[]{:S(2)}) copy-start(s32[128,12]{0,1:T(8,128)} %param.12) | copy-start | bytes 18436
  7.2 10.0 %copy-start.5 = (bf16[1,128,1024]{2,1,0:T(8,128)(2,1)S(1)}, bf16[1,128,1024]{2,1,0:T(8,128)(2,1)}, u32[]{:S(2)}) copy-start(bf16[1,128,1024]{2,1,0:T(8,128)(2,1)} %param.7) | copy-start | bytes 786436
  11.2 6.6 %copy-start.8 = (bf16[1,128,1024]{2,1,0:T(8,128)(2,1)S(1)}, bf16[1,128,1024]{2,1,0:T(8,128)(2,1)}, u32[]{:S(2)}) copy-start(bf16[1,128,1024]{2,1,0:T(8,128)(2,1)} %param.9) | copy-start | bytes 786436
  12.7 10.8 %all-to-all-start = ((bf16[4,16,2048]{2,1,0:T(8,128)(2,1)}), bf16[4,16,2048]{2,1,0:T(8,128)(2,1)}, u32[]{:S(2)}, u32[]{:S(2)}) async-start(bf16[4,16,2048]{2,1,0:T(8,128)(2,1)} %bitcast.6), calls=%async_computation | async-start | bytes 524288 | tf_op jit(solution)/shard_map/all_to_all | solution.py:67
  17.0 101.6 %reduce-scatter.9.cloned.1.call-start = ((), (), s32[]{:S(2)}) async-start(), calls=%async_computation.6 | async-start | bytes 2621440 | tf_op jit(solution)/shard_map/reduce_scatter | solution.py:110
  17.9 5.6 %copy-start.3 = (bf16[128,1024]{0,1:T(8,128)(2,1)}, bf16[128,1024]{0,1:T(8,128)(2,1)S(1)}, u32[]{:S(2)}) copy-start(bf16[128,1024]{0,1:T(8,128)(2,1)S(1)} %copy.28) | copy-start | bytes 786436
  18.1 5.5 %copy-start.1 = (bf16[1,128,1024]{1,2,0:T(8,128)(2,1)}, bf16[1,128,1024]{1,2,0:T(8,128)(2,1)S(1)}, u32[]{:S(2)}) copy-start(bf16[1,128,1024]{1,2,0:T(8,128)(2,1)S(1)} %copy.30) | copy-start | bytes 786436
  72.4 0.6 copy-start.7
  84.1 3.7 %copy-start.4 = (bf16[128,1024]{0,1:T(8,128)(2,1)S(1)}, bf16[128,1024]{0,1:T(8,128)(2,1)}, u32[]{:S(2)}) copy-start(bf16[128,1024]{0,1:T(8,128)(2,1)} %copy-done.3) | copy-start | bytes 786436
  91.2 3.1 %copy-start.2 = (bf16[1,128,1024]{1,2,0:T(8,128)(2,1)S(1)}, bf16[1,128,1024]{1,2,0:T(8,128)(2,1)}, u32[]{:S(2)}) copy-start(bf16[1,128,1024]{1,2,0:T(8,128)(2,1)} %copy-done.1) | copy-start | bytes 786436
  94.3 16.8 %copy-start.6 = (bf16[1,64,1024]{2,1,0:T(8,128)(2,1)S(1)}, bf16[1,64,1024]{2,1,0:T(8,128)(2,1)}, u32[]{:S(2)}) copy-start(bf16[1,64,1024]{2,1,0:T(8,128)(2,1)} %param.8) | copy-start | bytes 393220
  97.1 12.4 %all-to-all-start.1 = ((bf16[4,16,2048]{2,1,0:T(8,128)(2,1)}), bf16[4,16,2048]{2,1,0:T(8,128)(2,1)S(1)}, u32[]{:S(2)}, u32[]{:S(2)}) async-start(bf16[4,16,2048]{2,1,0:T(8,128)(2,1)} %bitcast.29), calls=%async_computation.1 | async-start | bytes 524288 | tf_op jit(solution)/shard_map/all_to_all | solution.py:84
  100.5 64.9 %reduce-scatter.11.cloned.1.call-start = ((), (), s32[]{:S(2)}) async-start(), calls=%async_computation.7 | async-start | bytes 5242880 | tf_op jit(solution)/shard_map/reduce_scatter | solution.py:113
  114.4 75.8 %reduce-scatter.13.cloned.1.call-start = ((), (), s32[]{:S(2)}) async-start(), calls=%async_computation.8 | async-start | bytes 655360
  120.6 97.3 %reduce-scatter.15.cloned.1.call-start = ((), (), s32[]{:S(2)}) async-start(), calls=%async_computation.9 | async-start | bytes 1310720
Sparse Core Ops, SparseCore 0:
  83.5 35.0 reduce-scatter.8
  121.1 44.3 reduce-scatter.10
  168.3 21.8 reduce-scatter.12
  192.4 25.4 reduce-scatter.14
where the time goes:
time: 228 us; the launch traced here: 227 us
  waiting for transfers between devices  105 us (46%)
  local copies, waits for them, and re-layouts  55 us (24%)
  matrix products  24.8 us (11%)
  other arithmetic  20.2 us (9%)
  between operations  14.1 us (6%)
  starting transfers between devices  7.8 us (3%)
    reduce_scatter x1, waiting for transfers between devices, per_device(): lax.psum_scatter(term_kv.astype(jnp.bfloat16), 'mp', scatter_dimension=0,...  44.8 us
    unnamed x6, waiting for transfers between devices  42.5 us
    unnamed x31, local copies, waits for them, and re-layouts  24.4 us
    gather x2, local copies, waits for them, and re-layouts, block_grads(): edges = table[ids]  17.7 us
    unnamed x5, other arithmetic  9.99 us
    all_to_all x1, waiting for transfers between devices, per_device(): lax.all_to_all(partial_value[:slots].reshape(count_mp, -1, 2 * width), 'm...  8.9 us
    slice x1, local copies, waits for them, and re-layouts, block_grads(): values_bf = edges[:, :, width:].reshape(count, nbrs, HEADS, -1)  6.28 us
  transfers between devices with their start and end apart: 6, of which 6 were waited for; matrix products, arithmetic and copies ran while one was open for 14% of the time, Pallas kernels for 0%

commit v1 on v0

v1 whole, which is shorter than its diff:
```python
import functools
import math

import jax
import jax.numpy as jnp
from jax import lax
from jax.experimental import pallas as pl
from jax.experimental.pallas import tpu as pltpu
from jax.sharding import PartitionSpec as P

HEADS = 16
LANES = 128
MESH = pl.DeviceIdType.MESH
F32 = jnp.float32
BF16 = jnp.bfloat16


def dot_nn(x, y):
    return lax.dot_general(x, y, (((1,), (0,)), ((), ())), preferred_element_type=F32)


def dot_nt(x, y):
    return lax.dot_general(x, y, (((1,), (1,)), ((), ())), preferred_element_type=F32)


def dot_tn(x, y):
    return lax.dot_general(x, y, (((0,), (0,)), ((), ())), preferred_element_type=F32)


def kernel(
    n, nd, wscale,
    gf, nf, cot, wq_h, wkv_h, nbr, sr_col, sr_row,
    dgrid, dnodes, dwq, dwkv,
    wq, wkv, out_feat, tab, q_s, kv_s, count_s, gf_all, nf_all, dq_s, dq_all,
    part_s, ret_s, dkv_s, dkv_all, tq, tkv, rq, rkv, oq, okv, swq, swkv,
    local_sem, feat_ss, feat_rs, half_ss, half_rs, dq_ss, dq_rs, ret_ss, ret_rs,
    dkv_ss, dkv_rs, z_ss, z_rs, sw_ss, sw_rs,
):
    grid_dev, width = gf.shape
    nodes = nf.shape[0]
    slots = sr_col.shape[0]
    rows = slots + nodes
    cap = slots // n
    nbrs = nbr.shape[1]
    a = width // gf_all.shape[2]
    b = n // a
    high = width // a
    wide = width // b
    out_rows = dwq.shape[0]
    head = width // HEADS
    per = LANES // head
    scale = head ** (-0.5)
    me = lax.axis_index("mp")
    zd = lax.axis_index("dp")
    mine_i = me // b
    mine_j = lax.rem(me, b)

    def to_mp(src, dst, ssem, rsem, peer):
        return pltpu.make_async_remote_copy(
            src_ref=src, dst_ref=dst, send_sem=ssem, recv_sem=rsem,
            device_id={"mp": peer}, device_id_type=MESH,
        )

    def to_dp(src, dst, ssem, rsem, peer):
        return pltpu.make_async_remote_copy(
            src_ref=src, dst_ref=dst, send_sem=ssem, recv_sem=rsem,
            device_id={"dp": peer}, device_id_type=MESH,
        )

    def peer_of(o):
        return lax.rem(me + o, n)

    load_q = pltpu.make_async_copy(wq_h, wq, local_sem.at[0])
    load_kv = pltpu.make_async_copy(wkv_h, wkv, local_sem.at[1])
    load_q.start()
    load_kv.start()
    barrier = pltpu.get_barrier_semaphore()
    for o in range(1, n):
        pl.semaphore_signal(barrier, inc=1, device_id={"mp": peer_of(o)}, device_id_type=MESH)
    for o in range(1, nd):
        pl.semaphore_signal(
            barrier, inc=1, device_id={"dp": lax.rem(zd + o, nd)}, device_id_type=MESH
        )
    pick = (sr_col[...] == lax.broadcasted_iota(jnp.int32, (slots, nodes), 1)).astype(BF16)
    out_feat[...] = dot_nn(pick, nf[...]).astype(BF16)
    tab[pl.ds(slots, nodes), :] = nf[...]
    own_slots = pl.ds(pl.multiple_of(me * cap, cap), cap)
    tab[own_slots, :] = jnp.zeros((cap, width), BF16)
    for jb in range(b):
        ret_s[jb, own_slots, :] = jnp.zeros((cap, 2 * wide), BF16)
    pl.semaphore_wait(barrier, n - 1 + nd - 1)

    feat = []
    for o in range(1, n):
        there = pl.ds(pl.multiple_of(peer_of(o) * cap, cap), cap)
        feat.append(
            to_mp(out_feat.at[there], tab.at[own_slots], feat_ss.at[o], feat_rs.at[o], peer_of(o))
        )
        feat[-1].start()

    ids = nbr[...]
    row_id = lax.broadcasted_iota(jnp.int32, (grid_dev, rows), 1)
    count = jnp.zeros((grid_dev, rows), F32)
    for k in range(nbrs):
        count += (ids[:, k : k + 1] == row_id).astype(F32)
    for s in range(per):
        count_s[s * grid_dev : (s + 1) * grid_dev, :] = count
    half_cols = pl.ds(pl.multiple_of(mine_i * high, high), high)
    gf_all[me] = gf[:, half_cols]
    nf_all[me] = nf[:, half_cols]
    load_q.wait()
    q_s[...] = dot_nn(gf[...], wq[...]).astype(BF16)
    for c in feat:
        c.wait_recv()
    half = []
    for o in range(1, n):
        there = pl.ds(pl.multiple_of((peer_of(o) // b) * high, high), high)
        half.append(
            to_mp(nf.at[:, there], nf_all.at[me], half_ss.at[0, o], half_rs.at[0, o], peer_of(o))
        )
        half.append(
            to_mp(gf.at[:, there], gf_all.at[me], half_ss.at[1, o], half_rs.at[1, o], peer_of(o))
        )
    for c in half:
        c.start()
    load_kv.wait()
    kv_s[...] = dot_nn(tab[...], wkv[...]).astype(BF16)

    lane = lax.broadcasted_iota(jnp.int32, (1, LANES), 1)
    keep = [(lane // head) == s for s in range(per)]

    def spread(x):
        return jnp.concatenate([jnp.where(m, x, jnp.zeros_like(x)) for m in keep], axis=0)

    dq_copies = []
    ret_copies = []
    for jb in range(b):

        def one(blk, carry):
            off = pl.multiple_of(jb * wide + blk * LANES, LANES)
            at = pl.ds(off, LANES)
            at_v = pl.ds(pl.multiple_of(width + off, LANES), LANES)
            here = pl.ds(pl.multiple_of(blk * LANES, LANES), LANES)
            here_v = pl.ds(pl.multiple_of(wide + blk * LANES, LANES), LANES)
            qs = spread(q_s[:, at])
            cs = spread(cot[:, at])
            keys = kv_s[:, at]
            values = kv_s[:, at_v]
            times = count_s[...]
            scores = dot_nt(qs, keys) * scale
            d_attn = dot_nt(cs, values)
            top = jnp.max(
                jnp.where(times > 0, scores, -jnp.inf), axis=1, keepdims=True
            )
            e = jnp.where(times > 0, times * jnp.exp(jnp.minimum(scores - top, 0.0)), 0.0)
            attn = e / jnp.sum(e, axis=1, keepdims=True)
            ds = attn * (d_attn - jnp.sum(attn * d_attn, axis=1, keepdims=True)) * scale
            ds = ds.astype(BF16)
            attn = attn.astype(BF16)
            dq = None
            for s in range(per):
                term = dot_nn(
                    ds[s * grid_dev : (s + 1) * grid_dev],
                    jnp.where(keep[s], keys, jnp.zeros_like(keys)),
                )
                dq = term if dq is None else dq + term
            dq_s[jb, :, here] = dq.astype(BF16)
            part_s[jb, :, here] = dot_tn(ds, qs).astype(BF16)
            part_s[jb, :, here_v] = dot_tn(attn, cs).astype(BF16)
            return carry

        lax.fori_loop(0, wide // LANES, one, 0)
        for o in range(1, n):
            peer = peer_of(o)
            c = to_mp(dq_s.at[jb], dq_all.at[me], dq_ss.at[o], dq_rs.at[o], peer)

            @pl.when(lax.rem(peer, b) == jb)
            def _():
                c.start()

        for o in range(1, n):
            there = pl.ds(pl.multiple_of(peer_of(o) * cap, cap), cap)
            c = to_mp(
                part_s.at[jb, there], ret_s.at[jb, own_slots],
                ret_ss.at[jb, o], ret_rs.at[jb, o], peer_of(o),
            )
            c.start()
            ret_copies.append(c)

    dq_all[me] = dq_s[mine_j]
    acc = None
    for jb in range(b):
        term = dot_nt(dq_s[jb], wq[:, jb * wide : (jb + 1) * wide])
        acc = term if acc is None else acc + term
    dgrid[...] = acc.astype(BF16)

    place = (sr_row[...] == lax.broadcasted_iota(jnp.int32, (nodes, slots), 0)).astype(BF16)
    for jb in range(b):
        for o in range(1, n):
            ret_copies[jb * (n - 1) + o - 1].wait_recv()
        dkv = part_s[jb, slots:, :].astype(F32) + dot_nn(place, ret_s[jb])
        dkv_s[jb] = dkv.astype(BF16)
        for o in range(1, n):
            peer = peer_of(o)
            c = to_mp(dkv_s.at[jb], dkv_all.at[me], dkv_ss.at[o], dkv_rs.at[o], peer)

            @pl.when(lax.rem(peer, b) == jb)
            def _():
                c.start()

    dkv_all[me] = dkv_s[mine_j]

    def got(src, dst, ssem, rsem):
        return to_mp(src, dst, ssem, rsem, peer_of(1))

    for c in half:
        c.wait_recv()
    for o in range(1, n):
        got(dq_s.at[0], dq_all.at[me], dq_ss.at[o], dq_rs.at[o]).wait_recv()
    term_q = dot_tn(
        gf_all[...].reshape(n * grid_dev, high), dq_all[...].reshape(n * grid_dev, wide)
    ) * wscale
    term_q = term_q.astype(BF16).reshape(b, nd, out_rows, wide)
    for d in range(nd):
        tq[d] = term_q[:, d]
    z_copies = []
    for o in range(1, nd):
        peer = lax.rem(zd + o, nd)
        z_copies.append(to_dp(tq.at[peer], rq.at[o], z_ss.at[0, o], z_rs.at[0, o], peer))
        z_copies[-1].start()

    acc = None
    for jb in range(b):
        for k in range(2):
            term = dot_nt(
                dkv_s[jb, :, k * wide : (k + 1) * wide],
                wkv[:, k * width + jb * wide : k * width + (jb + 1) * wide],
            )
            acc = term if acc is None else acc + term
    dnodes[...] = acc.astype(BF16)

    for o in range(1, n):
        got(dkv_s.at[0], dkv_all.at[me], dkv_ss.at[o], dkv_rs.at[o]).wait_recv()
    term_kv = dot_tn(
        nf_all[...].reshape(n * nodes, high), dkv_all[...].reshape(n * nodes, 2 * wide)
    ) * wscale
    term_kv = term_kv.astype(BF16).reshape(b, nd, out_rows, 2 * wide)
    for d in range(nd):
        tkv[d] = term_kv[:, d]
    for o in range(1, nd):
        peer = lax.rem(zd + o, nd)
        z_copies.append(to_dp(tkv.at[peer], rkv.at[o], z_ss.at[1, o], z_rs.at[1, o], peer))
        z_copies[-1].start()

    def finish(which, t, r, out, sw, width_out):
        total = t[zd].astype(F32)
        for o in range(1, nd):
            z_copies[which * (nd - 1) + o - 1].wait_recv()
            total += r[o].astype(F32)
        out[...] = total.astype(BF16)
        sent = []
        for o in range(1, b):
            mate = lax.rem(mine_j + o, b)
            c = to_mp(
                out.at[mate], sw.at[o], sw_ss.at[which, o], sw_rs.at[which, o],
                mine_i * b + mate,
            )
            c.start()
            sent.append(c)
        return sent

    sent_q = finish(0, tq, rq, oq, swq, wide)
    sent_kv = finish(1, tkv, rkv, okv, swkv, 2 * wide)

    def columns(j, k):
        return pl.ds(pl.multiple_of(k * width + j * wide, LANES), wide)

    dwq[:, columns(mine_j, 0)] = oq[mine_j].astype(F32)
    for o in range(1, b):
        source = lax.rem(mine_j + b - o, b)
        sent_q[o - 1].wait_recv()
        dwq[:, columns(source, 0)] = swq[o].astype(F32)
    for k in range(2):
        dwkv[:, columns(mine_j, k)] = okv[mine_j][:, k * wide : (k + 1) * wide].astype(F32)
    for o in range(1, b):
        source = lax.rem(mine_j + b - o, b)
        sent_kv[o - 1].wait_recv()
        for k in range(2):
            dwkv[:, columns(source, k)] = swkv[o][:, k * wide : (k + 1) * wide].astype(F32)

    for c in feat + half + ret_copies + z_copies + sent_q + sent_kv:
        c.wait_send()
    for o in range(1, n):
        got(dq_s.at[0], dq_all.at[me], dq_ss.at[o], dq_rs.at[o]).wait_send()
        got(dkv_s.at[0], dkv_all.at[me], dkv_ss.at[o], dkv_rs.at[o]).wait_send()


def per_device(grid_feat, node_feat, cotangent, w_query, w_keyval, neighbours, send_rows):
    n = lax.axis_size("mp")
    nd = lax.axis_size("dp")
    samples_dev, grid_dev, width = grid_feat.shape
    nodes = node_feat.shape[1]
    cap = send_rows.shape[2]
    slots = n * cap
    rows = slots + nodes
    a = 2
    b = n // a
    high = width // a
    wide = width // b
    out_rows = width // (n * nd)
    per = LANES * HEADS // width
    wscale = 1.0 / math.sqrt(samples_dev * nd * grid_dev * n)
    vmem = pl.BlockSpec(memory_space=pltpu.VMEM)
    anywhere = pl.BlockSpec(memory_space=pl.ANY)
    dma = pltpu.SemaphoreType.DMA
    d_grid, d_nodes, dw_query, dw_keyval = pl.pallas_call(
        functools.partial(kernel, n, nd, wscale),
        out_shape=(
            jax.ShapeDtypeStruct((grid_dev, width), BF16),
            jax.ShapeDtypeStruct((nodes, width), BF16),
            jax.ShapeDtypeStruct((out_rows, width), F32),
            jax.ShapeDtypeStruct((out_rows, 2 * width), F32),
        ),
        in_specs=[vmem, vmem, vmem, anywhere, anywhere, vmem, vmem, vmem],
        out_specs=(vmem, vmem, vmem, vmem),
        scratch_shapes=[
            pltpu.VMEM((width, width), BF16),
            pltpu.VMEM((width, 2 * width), BF16),
            pltpu.VMEM((slots, width), BF16),
            pltpu.VMEM((rows, width), BF16),
            pltpu.VMEM((grid_dev, width), BF16),
            pltpu.VMEM((rows, 2 * width), BF16),
            pltpu.VMEM((per * grid_dev, rows), F32),
            pltpu.VMEM((n, grid_dev, high), BF16),
            pltpu.VMEM((n, nodes, high), BF16),
            pltpu.VMEM((b, grid_dev, wide), BF16),
            pltpu.VMEM((n, grid_dev, wide), BF16),
            pltpu.VMEM((b, rows, 2 * wide), BF16),
            pltpu.VMEM((b, slots, 2 * wide), BF16),
            pltpu.VMEM((b, nodes, 2 * wide), BF16),
            pltpu.VMEM((n, nodes, 2 * wide), BF16),
            pltpu.VMEM((nd, b, out_rows, wide), BF16),
            pltpu.VMEM((nd, b, out_rows, 2 * wide), BF16),
            pltpu.VMEM((nd, b, out_rows, wide), BF16),
            pltpu.VMEM((nd, b, out_rows, 2 * wide), BF16),
            pltpu.VMEM((b, out_rows, wide), BF16),
            pltpu.VMEM((b, out_rows, 2 * wide), BF16),
            pltpu.VMEM((b, out_rows, wide), BF16),
            pltpu.VMEM((b, out_rows, 2 * wide), BF16),
            dma((2,)),
            dma((n,)), dma((n,)),
            dma((2, n)), dma((2, n)),
            dma((n,)), dma((n,)),
            dma((b, n)), dma((b, n)),
            dma((n,)), dma((n,)),
            dma((2, nd)), dma((2, nd)),
            dma((2, b)), dma((2, b)),
        ],
        compiler_params=pltpu.CompilerParams(
            collective_id=0, has_side_effects=True, vmem_limit_bytes=56 * 1024 * 1024
        ),
        name="graph_attention_grads",
    )(
        grid_feat[0], node_feat[0], cotangent[0], w_query, w_keyval, neighbours,
        send_rows.reshape(slots, 1), send_rows.reshape(1, slots),
    )
    return d_grid[None], d_nodes[None], dw_query, dw_keyval


def solution(mesh):
    in_specs = (
        P(("groups", "dp"), "mp", None),
        P(("groups", "dp"), "mp", None),
        P(("groups", "dp"), "mp", None),
        P(),
        P(),
        P("mp", None),
        P("mp", None, None),
    )
    out_specs = (
        P(("groups", "dp"), "mp", None),
        P(("groups", "dp"), "mp", None),
        P(("groups", "mp", "dp"), None),
        P(("groups", "mp", "dp"), None),
    )
    return jax.shard_map(
        per_device, mesh=mesh, in_specs=in_specs, out_specs=out_specs, check_vma=False
    )
```

time: 228 us -> 77.1 us (0.34)
  the two profiles are of different devices: /device:TPU:0 before, /device:TPU:11 now
where the time goes in v1:
time: 77.1 us; the launch traced here: 76.7 us
  Pallas kernels  65.2 us (85%)
  local copies, waits for them, and re-layouts  10.9 us (14%)
    pallas_call x1, Pallas kernels, per_device(): pl.pallas_call(functools.partial(kernel, n, nd, wscale), out_shape=(jax.S...  65.2 us
    unnamed x5, local copies, waits for them, and re-layouts  8.21 us

profile of v1, /device:TPU:11, one launch (start us, length us, event | category | flops | bytes accessed | tf_op | source)
XLA Modules:
  0.0 76.7 jit_solution(5378796269474288767)
XLA Ops:
  0.6 1.3 %reshape.15.sr_row = s32[1,64]{1,0:T(1,128)} reshape(s32[1,4,16]{2,1,0:T(4,128)} %param.13) | data formatting | bytes 512 | tf_op jit(solution)/shard_map/reshape | solution.py:365
  1.9 1.4 %reshape.16.sr_col = s32[64,1]{1,0:T(8,128)} reshape(s32[1,4,16]{2,1,0:T(4,128)} %param.13) | data formatting | bytes 512 | tf_op jit(solution)/shard_map/reshape | solution.py:365
  3.3 1.4 %copy.11.nbr = s32[128,12]{1,0:T(8,128)} copy(s32[128,12]{0,1:T(8,128)} %param.12) | data formatting | bytes 12288 | tf_op args[5]
  4.7 65.2 %graph_attention_grads.1 = (bf16[128,1024]{1,0:T(8,128)(2,1)}, bf16[64,1024]{1,0:T(8,128)(2,1)}, f32[64,1024]{1,0:T(8,128)}, f32[64,2048]{1,0:T(8,128)}) custom-call(bf16[128,1024]{1,0:T(8,128)(2,1)} %bitcast.5, bf16[64,1024]{1,0:T(8,128)(2,1)} %bitcast.8, bf16[128,1024]{1,0:T(8,128)(2,1)} %bitcast.6, bf16[1024,1024]{1,0:T(8,128)(2,1)} %wq_h.1, ...), custom_call_target="tpu_custom_call" | custom-call | tf_op jit(solution)/shard_map/graph_attention_grads/pallas_call | solution.py:316
  70.0 1.7 %copy.17 = bf16[1,128,1024]{2,1,0:T(8,128)(2,1)} copy(bf16[1,128,1024]{2,1,0:T(8,128)(2,1)} %bitcast.7) | data formatting | bytes 524288
  71.6 1.6 %copy.18 = bf16[1,64,1024]{2,1,0:T(8,128)(2,1)} copy(bf16[1,64,1024]{2,1,0:T(8,128)(2,1)} %bitcast.9) | data formatting | bytes 262144
  73.2 1.7 %copy.19 = f32[64,1024]{1,0:T(8,128)} copy(f32[64,1024]{1,0:T(8,128)} %get-tuple-element.18) | data formatting | bytes 524288
  74.9 1.9 %copy.20 = f32[64,2048]{1,0:T(8,128)} copy(f32[64,2048]{1,0:T(8,128)} %get-tuple-element.19) | data formatting | bytes 1048576

commit v2 on v1

--- a/solution.py
+++ b/solution.py
@@ -29,19 +29,19 @@
 
 def kernel(
     n, nd, wscale,
-    gf, nf, cot, wq_h, wkv_h, nbr, sr_col, sr_row,
+    gf, nf, cot, wq_h, wkv_h, nbr, sr,
     dgrid, dnodes, dwq, dwkv,
     wq, wkv, out_feat, tab, q_s, kv_s, count_s, gf_all, nf_all, dq_s, dq_all,
-    part_s, ret_s, dkv_s, dkv_all, tq, tkv, rq, rkv, oq, okv, swq, swkv,
+    part_s, ret_s, dkv_s, dkv_all, tq, tkv, rq, rkv, sq, skv, oq, okv, swq, swkv, place_s,
     local_sem, feat_ss, feat_rs, half_ss, half_rs, dq_ss, dq_rs, ret_ss, ret_rs,
     dkv_ss, dkv_rs, z_ss, z_rs, sw_ss, sw_rs,
 ):
     grid_dev, width = gf.shape
     nodes = nf.shape[0]
-    slots = sr_col.shape[0]
+    slots = out_feat.shape[0]
     rows = slots + nodes
     cap = slots // n
-    nbrs = nbr.shape[1]
+    nbrs = nbr.shape[0]
     a = width // gf_all.shape[2]
     b = n // a
     high = width // a
@@ -81,8 +81,11 @@
         pl.semaphore_signal(
             barrier, inc=1, device_id={"dp": lax.rem(zd + o, nd)}, device_id_type=MESH
         )
-    pick = (sr_col[...] == lax.broadcasted_iota(jnp.int32, (slots, nodes), 1)).astype(BF16)
-    out_feat[...] = dot_nn(pick, nf[...]).astype(BF16)
+    node_id = lax.broadcasted_iota(jnp.int32, (nodes, cap), 0)
+    for p in range(n):
+        place_s[:, p * cap : (p + 1) * cap] = (sr[p : p + 1, :] == node_id).astype(F32)
+    place = place_s[...].astype(BF16)
+    out_feat[...] = dot_tn(place, nf[...]).astype(BF16)
     tab[pl.ds(slots, nodes), :] = nf[...]
     own_slots = pl.ds(pl.multiple_of(me * cap, cap), cap)
     tab[own_slots, :] = jnp.zeros((cap, width), BF16)
@@ -99,10 +102,11 @@
         feat[-1].start()
 
     ids = nbr[...]
-    row_id = lax.broadcasted_iota(jnp.int32, (grid_dev, rows), 1)
-    count = jnp.zeros((grid_dev, rows), F32)
+    row_id = lax.broadcasted_iota(jnp.int32, (rows, grid_dev), 0)
+    count = jnp.zeros((rows, grid_dev), F32)
     for k in range(nbrs):
-        count += (ids[:, k : k + 1] == row_id).astype(F32)
+        count += (ids[k : k + 1, :] == row_id).astype(F32)
+    count = count.T
     for s in range(per):
         count_s[s * grid_dev : (s + 1) * grid_dev, :] = count
     half_cols = pl.ds(pl.multiple_of(mine_i * high, high), high)
@@ -194,7 +198,6 @@
         acc = term if acc is None else acc + term
     dgrid[...] = acc.astype(BF16)
 
-    place = (sr_row[...] == lax.broadcasted_iota(jnp.int32, (nodes, slots), 0)).astype(BF16)
     for jb in range(b):
         for o in range(1, n):
             ret_copies[jb * (n - 1) + o - 1].wait_recv()
@@ -223,11 +226,40 @@
     term_q = term_q.astype(BF16).reshape(b, nd, out_rows, wide)
     for d in range(nd):
         tq[d] = term_q[:, d]
-    z_copies = []
-    for o in range(1, nd):
-        peer = lax.rem(zd + o, nd)
-        z_copies.append(to_dp(tq.at[peer], rq.at[o], z_ss.at[0, o], z_rs.at[0, o], peer))
-        z_copies[-1].start()
+
+    def hops(which, t, r):
+        found = []
+        for step in range(1, nd):
+            for way in range(2):
+                d = nd - step if way == 0 else step - 1
+                ahead = jnp.minimum(zd + 1, nd - 1) if way == 0 else jnp.maximum(zd - 1, 0)
+                c = to_dp(
+                    t.at[d], r.at[way, d], z_ss.at[which, way, d], z_rs.at[which, way, d], ahead
+                )
+                sends = zd < d if way == 0 else zd > d
+                first = zd == 0 if way == 0 else zd == nd - 1
+                found.append((c, sends, first, way, d))
+        return found
+
+    def lead(found):
+        for c, sends, first, way, d in found:
+
+            @pl.when(jnp.logical_and(sends, first))
+            def _():
+                c.start()
+
+    def relay(found, t, r):
+        for c, sends, first, way, d in found:
+
+            @pl.when(jnp.logical_and(sends, jnp.logical_not(first)))
+            def _():
+                c.wait_recv()
+                t[d] = (t[d].astype(F32) + r[way, d].astype(F32)).astype(BF16)
+                c.start()
+
+    hops_q = hops(0, tq, rq)
+    hops_kv = hops(1, tkv, rkv)
+    lead(hops_q)
 
     acc = None
     for jb in range(b):
@@ -247,17 +279,22 @@
     term_kv = term_kv.astype(BF16).reshape(b, nd, out_rows, 2 * wide)
     for d in range(nd):
         tkv[d] = term_kv[:, d]
-    for o in range(1, nd):
-        peer = lax.rem(zd + o, nd)
-        z_copies.append(to_dp(tkv.at[peer], rkv.at[o], z_ss.at[1, o], z_rs.at[1, o], peer))
-        z_copies[-1].start()
-
-    def finish(which, t, r, out, sw, width_out):
-        total = t[zd].astype(F32)
-        for o in range(1, nd):
-            z_copies[which * (nd - 1) + o - 1].wait_recv()
-            total += r[o].astype(F32)
-        out[...] = total.astype(BF16)
+    lead(hops_kv)
+    relay(hops_q, tq, rq)
+
+    def finish(which, t, r, total, out, sw):
+        total[...] = t[zd].astype(F32)
+        for way in range(2):
+
+            @pl.when(zd > 0 if way == 0 else zd < nd - 1)
+            def _():
+                to_dp(
+                    t.at[0], r.at[way, zd], z_ss.at[which, way, zd], z_rs.at[which, way, zd],
+                    lax.rem(zd + 1, nd),
+                ).wait_recv()
+                total[...] += r[way, zd].astype(F32)
+
+        out[...] = total[...].astype(BF16)
         sent = []
         for o in range(1, b):
             mate = lax.rem(mine_j + o, b)
@@ -269,30 +306,44 @@
             sent.append(c)
         return sent
 
-    sent_q = finish(0, tq, rq, oq, swq, wide)
-    sent_kv = finish(1, tkv, rkv, okv, swkv, 2 * wide)
+    sent_q = finish(0, tq, rq, sq, oq, swq)
+    relay(hops_kv, tkv, rkv)
+    sent_kv = finish(1, tkv, rkv, skv, okv, swkv)
 
     def columns(j, k):
         return pl.ds(pl.multiple_of(k * width + j * wide, LANES), wide)
 
-    dwq[:, columns(mine_j, 0)] = oq[mine_j].astype(F32)
+    dwq[:, columns(mine_j, 0)] = oq[mine_j]
     for o in range(1, b):
         source = lax.rem(mine_j + b - o, b)
         sent_q[o - 1].wait_recv()
-        dwq[:, columns(source, 0)] = swq[o].astype(F32)
+        dwq[:, columns(source, 0)] = swq[o]
     for k in range(2):
-        dwkv[:, columns(mine_j, k)] = okv[mine_j][:, k * wide : (k + 1) * wide].astype(F32)
+        dwkv[:, columns(mine_j, k)] = okv[mine_j][:, k * wide : (k + 1) * wide]
     for o in range(1, b):
         source = lax.rem(mine_j + b - o, b)
         sent_kv[o - 1].wait_recv()
         for k in range(2):
-            dwkv[:, columns(source, k)] = swkv[o][:, k * wide : (k + 1) * wide].astype(F32)
-
-    for c in feat + half + ret_copies + z_copies + sent_q + sent_kv:
+            dwkv[:, columns(source, k)] = swkv[o][:, k * wide : (k + 1) * wide]
+
+    for c in feat + half + ret_copies + sent_q + sent_kv:
         c.wait_send()
+    for c, sends, first, way, d in hops_q + hops_kv:
+
+        @pl.when(sends)
+        def _():
+            c.wait_send()
+
     for o in range(1, n):
         got(dq_s.at[0], dq_all.at[me], dq_ss.at[o], dq_rs.at[o]).wait_send()
         got(dkv_s.at[0], dkv_all.at[me], dkv_ss.at[o], dkv_rs.at[o]).wait_send()
+
+
+def write_out(d_grid, d_nodes, dw_query, dw_keyval, out_grid, out_nodes, out_q, out_kv):
+    out_grid[...] = d_grid[...]
+    out_nodes[...] = d_nodes[...]
+    out_q[...] = dw_query[...].astype(F32)
+    out_kv[...] = dw_keyval[...].astype(F32)
 
 
 def per_device(grid_feat, node_feat, cotangent, w_query, w_keyval, neighbours, send_rows):
@@ -318,10 +369,10 @@
         out_shape=(
             jax.ShapeDtypeStruct((grid_dev, width), BF16),
             jax.ShapeDtypeStruct((nodes, width), BF16),
-            jax.ShapeDtypeStruct((out_rows, width), F32),
-            jax.ShapeDtypeStruct((out_rows, 2 * width), F32),
+            jax.ShapeDtypeStruct((out_rows, width), BF16),
+            jax.ShapeDtypeStruct((out_rows, 2 * width), BF16),
         ),
-        in_specs=[vmem, vmem, vmem, anywhere, anywhere, vmem, vmem, vmem],
+        in_specs=[vmem, vmem, vmem, anywhere, anywhere, vmem, vmem],
         out_specs=(vmem, vmem, vmem, vmem),
         scratch_shapes=[
             pltpu.VMEM((width, width), BF16),
@@ -341,19 +392,22 @@
             pltpu.VMEM((n, nodes, 2 * wide), BF16),
             pltpu.VMEM((nd, b, out_rows, wide), BF16),
             pltpu.VMEM((nd, b, out_rows, 2 * wide), BF16),
-            pltpu.VMEM((nd, b, out_rows, wide), BF16),
-            pltpu.VMEM((nd, b, out_rows, 2 * wide), BF16),
+            pltpu.VMEM((2, nd, b, out_rows, wide), BF16),
+            pltpu.VMEM((2, nd, b, out_rows, 2 * wide), BF16),
+            pltpu.VMEM((b, out_rows, wide), F32),
+            pltpu.VMEM((b, out_rows, 2 * wide), F32),
             pltpu.VMEM((b, out_rows, wide), BF16),
             pltpu.VMEM((b, out_rows, 2 * wide), BF16),
             pltpu.VMEM((b, out_rows, wide), BF16),
             pltpu.VMEM((b, out_rows, 2 * wide), BF16),
+            pltpu.VMEM((nodes, slots), F32),
             dma((2,)),
             dma((n,)), dma((n,)),
             dma((2, n)), dma((2, n)),
             dma((n,)), dma((n,)),
             dma((b, n)), dma((b, n)),
             dma((n,)), dma((n,)),
-            dma((2, nd)), dma((2, nd)),
+            dma((2, 2, nd)), dma((2, 2, nd)),
             dma((2, b)), dma((2, b)),
         ],
         compiler_params=pltpu.CompilerParams(
@@ -361,9 +415,20 @@
         ),
         name="graph_attention_grads",
     )(
-        grid_feat[0], node_feat[0], cotangent[0], w_query, w_keyval, neighbours,
-        send_rows.reshape(slots, 1), send_rows.reshape(1, slots),
+        grid_feat[0], node_feat[0], cotangent[0], w_query, w_keyval, neighbours.T, send_rows[0],
     )
+    d_grid, d_nodes, dw_query, dw_keyval = pl.pallas_call(
+        write_out,
+        out_shape=(
+            jax.ShapeDtypeStruct((grid_dev, width), BF16),
+            jax.ShapeDtypeStruct((nodes, width), BF16),
+            jax.ShapeDtypeStruct((out_rows, width), F32),
+            jax.ShapeDtypeStruct((out_rows, 2 * width), F32),
+        ),
+        in_specs=[vmem, vmem, vmem, vmem],
+        out_specs=(vmem, vmem, vmem, vmem),
+        name="write_out",
+    )(d_grid, d_nodes, dw_query, dw_keyval)
     return d_grid[None], d_nodes[None], dw_query, dw_keyval
 
 

time: 77.1 us -> 73.4 us (0.952)
  the two profiles are of different devices: /device:TPU:11 before, /device:TPU:0 now
where the time goes in v2:
time: 73.4 us; the launch traced here: 73.2 us
  Pallas kernels  72.6 us (99%)
    pallas_call x1, Pallas kernels, per_device(): pl.pallas_call(functools.partial(kernel, n, nd, wscale), out_shape=(jax.S...  70.4 us
    pallas_call x1, Pallas kernels, per_device(): pl.pallas_call(write_out, out_shape=(jax.ShapeDtypeStruct((grid_dev, widt...  2.18 us

profile of v2, /device:TPU:0, one launch (start us, length us, event | category | flops | bytes accessed | tf_op | source)
XLA Modules:
  0.0 73.2 jit_solution(1396640821138918005)
XLA Ops:
  0.6 70.4 %graph_attention_grads.1 = (bf16[128,1024]{1,0:T(8,128)(2,1)}, bf16[64,1024]{1,0:T(8,128)(2,1)}, bf16[64,1024]{1,0:T(8,128)(2,1)}, bf16[64,2048]{1,0:T(8,128)(2,1)}) custom-call(bf16[128,1024]{1,0:T(8,128)(2,1)} %bitcast.7, bf16[64,1024]{1,0:T(8,128)(2,1)} %bitcast.9, bf16[128,1024]{1,0:T(8,128)(2,1)} %bitcast.8, bf16[1024,1024]{1,0:T(8,128)(2,1)} %wq_h.1, ...), custom_call_target="tpu_custom_call" | custom-call | tf_op jit(solution)/shard_map/graph_attention_grads/pallas_call | solution.py:367
  71.0 2.2 %write_out.1 = (bf16[128,1024]{1,0:T(8,128)(2,1)}, bf16[64,1024]{1,0:T(8,128)(2,1)}, f32[64,1024]{1,0:T(8,128)}, f32[64,2048]{1,0:T(8,128)}) custom-call(bf16[128,1024]{1,0:T(8,128)(2,1)} %get-tuple-element.12.d_grid, bf16[64,1024]{1,0:T(8,128)(2,1)} %get-tuple-element.13.d_nodes, bf16[64,1024]{1,0:T(8,128)(2,1)} %get-tuple-element.14.dw_query, ...), custom_call_target="tpu_custom_call" | custom-call | tf_op jit(solution)/shard_map/write_out/pallas_call | solution.py:420

commit v3 on v2

--- a/solution.py
+++ b/solution.py
@@ -100,6 +100,20 @@
             to_mp(out_feat.at[there], tab.at[own_slots], feat_ss.at[o], feat_rs.at[o], peer_of(o))
         )
         feat[-1].start()
+    half = []
+    for which, whole, parts in ((1, gf, gf_all), (0, nf, nf_all)):
+        for o in range(1, n):
+            there = pl.ds(pl.multiple_of((peer_of(o) // b) * high, high), high)
+            half.append(
+                to_mp(
+                    whole.at[:, there], parts.at[me],
+                    half_ss.at[which, o], half_rs.at[which, o], peer_of(o),
+                )
+            )
+            half[-1].start()
+    half_cols = pl.ds(pl.multiple_of(mine_i * high, high), high)
+    gf_all[me] = gf[:, half_cols]
+    nf_all[me] = nf[:, half_cols]
 
     ids = nbr[...]
     row_id = lax.broadcasted_iota(jnp.int32, (rows, grid_dev), 0)
@@ -109,24 +123,10 @@
     count = count.T
     for s in range(per):
         count_s[s * grid_dev : (s + 1) * grid_dev, :] = count
-    half_cols = pl.ds(pl.multiple_of(mine_i * high, high), high)
-    gf_all[me] = gf[:, half_cols]
-    nf_all[me] = nf[:, half_cols]
     load_q.wait()
     q_s[...] = dot_nn(gf[...], wq[...]).astype(BF16)
     for c in feat:
         c.wait_recv()
-    half = []
-    for o in range(1, n):
-        there = pl.ds(pl.multiple_of((peer_of(o) // b) * high, high), high)
-        half.append(
-            to_mp(nf.at[:, there], nf_all.at[me], half_ss.at[0, o], half_rs.at[0, o], peer_of(o))
-        )
-        half.append(
-            to_mp(gf.at[:, there], gf_all.at[me], half_ss.at[1, o], half_rs.at[1, o], peer_of(o))
-        )
-    for c in half:
-        c.start()
     load_kv.wait()
     kv_s[...] = dot_nn(tab[...], wkv[...]).astype(BF16)
 
@@ -175,14 +175,6 @@
 
         lax.fori_loop(0, wide // LANES, one, 0)
         for o in range(1, n):
-            peer = peer_of(o)
-            c = to_mp(dq_s.at[jb], dq_all.at[me], dq_ss.at[o], dq_rs.at[o], peer)
-
-            @pl.when(lax.rem(peer, b) == jb)
-            def _():
-                c.start()
-
-        for o in range(1, n):
             there = pl.ds(pl.multiple_of(peer_of(o) * cap, cap), cap)
             c = to_mp(
                 part_s.at[jb, there], ret_s.at[jb, own_slots],
@@ -190,14 +182,15 @@
             )
             c.start()
             ret_copies.append(c)
+        for o in range(1, n):
+            peer = peer_of(o)
+            c = to_mp(dq_s.at[jb], dq_all.at[me], dq_ss.at[o], dq_rs.at[o], peer)
+
+            @pl.when(lax.rem(peer, b) == jb)
+            def _():
+                c.start()
 
     dq_all[me] = dq_s[mine_j]
-    acc = None
-    for jb in range(b):
-        term = dot_nt(dq_s[jb], wq[:, jb * wide : (jb + 1) * wide])
-        acc = term if acc is None else acc + term
-    dgrid[...] = acc.astype(BF16)
-
     for jb in range(b):
         for o in range(1, n):
             ret_copies[jb * (n - 1) + o - 1].wait_recv()
@@ -212,6 +205,12 @@
                 c.start()
 
     dkv_all[me] = dkv_s[mine_j]
+
+    acc = None
+    for jb in range(b):
+        term = dot_nt(dq_s[jb], wq[:, jb * wide : (jb + 1) * wide])
+        acc = term if acc is None else acc + term
+    dgrid[...] = acc.astype(BF16)
 
     def got(src, dst, ssem, rsem):
         return to_mp(src, dst, ssem, rsem, peer_of(1))
@@ -227,34 +226,42 @@
     for d in range(nd):
         tq[d] = term_q[:, d]
 
+    far = nd // 2
+
+    def region(k, way):
+        if 2 * k == nd:
+            return slice(0, b // 2) if way == 0 else slice(b // 2, b)
+        return slice(0, b)
+
     def hops(which, t, r):
-        found = []
-        for step in range(1, nd):
+        found = {}
+        for k in range(far, 0, -1):
             for way in range(2):
-                d = nd - step if way == 0 else step - 1
-                ahead = jnp.minimum(zd + 1, nd - 1) if way == 0 else jnp.maximum(zd - 1, 0)
-                c = to_dp(
-                    t.at[d], r.at[way, d], z_ss.at[which, way, d], z_rs.at[which, way, d], ahead
+                d = lax.rem(zd + k, nd) if way == 0 else lax.rem(zd + nd - k, nd)
+                ahead = lax.rem(zd + 1, nd) if way == 0 else lax.rem(zd + nd - 1, nd)
+                piece = region(k, way)
+                found[k, way] = (
+                    to_dp(
+                        t.at[d, piece], r.at[way, k, piece],
+                        z_ss.at[which, way, k], z_rs.at[which, way, k], ahead,
+                    ),
+                    d,
                 )
-                sends = zd < d if way == 0 else zd > d
-                first = zd == 0 if way == 0 else zd == nd - 1
-                found.append((c, sends, first, way, d))
         return found
 
     def lead(found):
-        for c, sends, first, way, d in found:
-
-            @pl.when(jnp.logical_and(sends, first))
-            def _():
-                c.start()
+        for way in range(2):
+            found[far, way][0].start()
 
     def relay(found, t, r):
-        for c, sends, first, way, d in found:
-
-            @pl.when(jnp.logical_and(sends, jnp.logical_not(first)))
-            def _():
-                c.wait_recv()
-                t[d] = (t[d].astype(F32) + r[way, d].astype(F32)).astype(BF16)
+        for k in range(far - 1, 0, -1):
+            for way in range(2):
+                c, d = found[k, way]
+                found[k + 1, way][0].wait_recv()
+                piece = region(k + 1, way)
+                t[d, piece] = (t[d, piece].astype(F32) + r[way, k + 1, piece].astype(F32)).astype(
+                    BF16
+                )
                 c.start()
 
     hops_q = hops(0, tq, rq)
@@ -271,6 +278,7 @@
             acc = term if acc is None else acc + term
     dnodes[...] = acc.astype(BF16)
 
+    relay(hops_q, tq, rq)
     for o in range(1, n):
         got(dkv_s.at[0], dkv_all.at[me], dkv_ss.at[o], dkv_rs.at[o]).wait_recv()
     term_kv = dot_tn(
@@ -280,20 +288,13 @@
     for d in range(nd):
         tkv[d] = term_kv[:, d]
     lead(hops_kv)
-    relay(hops_q, tq, rq)
-
-    def finish(which, t, r, total, out, sw):
+
+    def finish(which, found, t, r, total, out, sw):
         total[...] = t[zd].astype(F32)
         for way in range(2):
-
-            @pl.when(zd > 0 if way == 0 else zd < nd - 1)
-            def _():
-                to_dp(
-                    t.at[0], r.at[way, zd], z_ss.at[which, way, zd], z_rs.at[which, way, zd],
-                    lax.rem(zd + 1, nd),
-                ).wait_recv()
-                total[...] += r[way, zd].astype(F32)
-
+            found[1, way][0].wait_recv()
+            piece = region(1, way)
+            total[piece] += r[way, 1, piece].astype(F32)
         out[...] = total[...].astype(BF16)
         sent = []
         for o in range(1, b):
@@ -306,9 +307,9 @@
             sent.append(c)
         return sent
 
-    sent_q = finish(0, tq, rq, sq, oq, swq)
+    sent_q = finish(0, hops_q, tq, rq, sq, oq, swq)
     relay(hops_kv, tkv, rkv)
-    sent_kv = finish(1, tkv, rkv, skv, okv, swkv)
+    sent_kv = finish(1, hops_kv, tkv, rkv, skv, okv, swkv)
 
     def columns(j, k):
         return pl.ds(pl.multiple_of(k * width + j * wide, LANES), wide)
@@ -328,12 +329,8 @@
 
     for c in feat + half + ret_copies + sent_q + sent_kv:
         c.wait_send()
-    for c, sends, first, way, d in hops_q + hops_kv:
-
-        @pl.when(sends)
-        def _():
-            c.wait_send()
-
+    for c, _ in list(hops_q.values()) + list(hops_kv.values()):
+        c.wait_send()
     for o in range(1, n):
         got(dq_s.at[0], dq_all.at[me], dq_ss.at[o], dq_rs.at[o]).wait_send()
         got(dkv_s.at[0], dkv_all.at[me], dkv_ss.at[o], dkv_rs.at[o]).wait_send()
@@ -392,8 +389,8 @@
             pltpu.VMEM((n, nodes, 2 * wide), BF16),
             pltpu.VMEM((nd, b, out_rows, wide), BF16),
             pltpu.VMEM((nd, b, out_rows, 2 * wide), BF16),
-            pltpu.VMEM((2, nd, b, out_rows, wide), BF16),
-            pltpu.VMEM((2, nd, b, out_rows, 2 * wide), BF16),
+            pltpu.VMEM((2, nd // 2 + 1, b, out_rows, wide), BF16),
+            pltpu.VMEM((2, nd // 2 + 1, b, out_rows, 2 * wide), BF16),
             pltpu.VMEM((b, out_rows, wide), F32),
             pltpu.VMEM((b, out_rows, 2 * wide), F32),
             pltpu.VMEM((b, out_rows, wide), BF16),
@@ -407,7 +404,7 @@
             dma((n,)), dma((n,)),
             dma((b, n)), dma((b, n)),
             dma((n,)), dma((n,)),
-            dma((2, 2, nd)), dma((2, 2, nd)),
+            dma((2, 2, nd // 2 + 1)), dma((2, 2, nd // 2 + 1)),
             dma((2, b)), dma((2, b)),
         ],
         compiler_params=pltpu.CompilerParams(

time: 73.4 us -> 60.1 us (0.82)
  Pallas kernels: 72.6 us -> 59.3 us
    pallas_call x1, Pallas kernels: 70.4 us -> 57.1 us  [per_device(): pl.pallas_call(functools.partial(kernel, n, nd, wscale), out_shape=(jax.S...]
where the time goes in v3:
time: 60.1 us; the launch traced here: 59.9 us
  Pallas kernels  59.3 us (99%)
  between operations  0.64 us (1%)
    pallas_call x1, Pallas kernels, per_device(): pl.pallas_call(functools.partial(kernel, n, nd, wscale), out_shape=(jax.S...  57.1 us
    pallas_call x1, Pallas kernels, per_device(): pl.pallas_call(write_out, out_shape=(jax.ShapeDtypeStruct((grid_dev, widt...  2.18 us

profile of v3, /device:TPU:0, one launch (start us, length us, event | category | flops | bytes accessed | tf_op | source)
XLA Modules:
  0.0 59.9 jit_solution(9728143924481869437)
XLA Ops:
  0.6 57.1 %graph_attention_grads.1 = (bf16[128,1024]{1,0:T(8,128)(2,1)}, bf16[64,1024]{1,0:T(8,128)(2,1)}, bf16[64,1024]{1,0:T(8,128)(2,1)}, bf16[64,2048]{1,0:T(8,128)(2,1)}) custom-call(bf16[128,1024]{1,0:T(8,128)(2,1)} %bitcast.7, bf16[64,1024]{1,0:T(8,128)(2,1)} %bitcast.9, bf16[128,1024]{1,0:T(8,128)(2,1)} %bitcast.8, bf16[1024,1024]{1,0:T(8,128)(2,1)} %wq_h.1, ...), custom_call_target="tpu_custom_call" | custom-call | tf_op jit(solution)/shard_map/graph_attention_grads/pallas_call | solution.py:364
  57.7 2.2 %write_out.1 = (bf16[128,1024]{1,0:T(8,128)(2,1)}, bf16[64,1024]{1,0:T(8,128)(2,1)}, f32[64,1024]{1,0:T(8,128)}, f32[64,2048]{1,0:T(8,128)}) custom-call(bf16[128,1024]{1,0:T(8,128)(2,1)} %get-tuple-element.12.d_grid, bf16[64,1024]{1,0:T(8,128)(2,1)} %get-tuple-element.13.d_nodes, bf16[64,1024]{1,0:T(8,128)(2,1)} %get-tuple-element.14.dw_query, ...), custom_call_target="tpu_custom_call" | custom-call | tf_op jit(solution)/shard_map/write_out/pallas_call | solution.py:417

commit v4 on v3

--- a/solution.py
+++ b/solution.py
@@ -100,18 +100,33 @@
             to_mp(out_feat.at[there], tab.at[own_slots], feat_ss.at[o], feat_rs.at[o], peer_of(o))
         )
         feat[-1].start()
+    half_cols = pl.ds(pl.multiple_of(mine_i * high, high), high)
+    other_i = lax.rem(mine_i + 1, a)
+    across = other_i * b + mine_j
+    other_cols = pl.ds(pl.multiple_of(other_i * high, high), high)
+    feature_sets = ((1, gf, gf_all), (0, nf, nf_all))
+
+    def mate_of(o):
+        return mine_i * b + lax.rem(mine_j + o, b)
+
+    crossing = []
     half = []
-    for which, whole, parts in ((1, gf, gf_all), (0, nf, nf_all)):
-        for o in range(1, n):
-            there = pl.ds(pl.multiple_of((peer_of(o) // b) * high, high), high)
+    for which, whole, parts in feature_sets:
+        crossing.append(
+            to_mp(
+                whole.at[:, other_cols], parts.at[me],
+                half_ss.at[which, 0], half_rs.at[which, 0], across,
+            )
+        )
+        crossing[-1].start()
+        for o in range(1, b):
             half.append(
                 to_mp(
-                    whole.at[:, there], parts.at[me],
-                    half_ss.at[which, o], half_rs.at[which, o], peer_of(o),
+                    whole.at[:, half_cols], parts.at[me],
+                    half_ss.at[which, o], half_rs.at[which, o], mate_of(o),
                 )
             )
             half[-1].start()
-    half_cols = pl.ds(pl.multiple_of(mine_i * high, high), high)
     gf_all[me] = gf[:, half_cols]
     nf_all[me] = nf[:, half_cols]
 
@@ -174,6 +189,17 @@
             return carry
 
         lax.fori_loop(0, wide // LANES, one, 0)
+        if jb == 0:
+            for c, (which, whole, parts) in zip(crossing, feature_sets):
+                c.wait_recv()
+                for o in range(1, b):
+                    half.append(
+                        to_mp(
+                            parts.at[across], parts.at[across],
+                            half_ss.at[which, b + o], half_rs.at[which, b + o], mate_of(o),
+                        )
+                    )
+                    half[-1].start()
         for o in range(1, n):
             there = pl.ds(pl.multiple_of(peer_of(o) * cap, cap), cap)
             c = to_mp(
@@ -327,7 +353,7 @@
         for k in range(2):
             dwkv[:, columns(source, k)] = swkv[o][:, k * wide : (k + 1) * wide]
 
-    for c in feat + half + ret_copies + sent_q + sent_kv:
+    for c in feat + crossing + half + ret_copies + sent_q + sent_kv:
         c.wait_send()
     for c, _ in list(hops_q.values()) + list(hops_kv.values()):
         c.wait_send()
@@ -400,7 +426,7 @@
             pltpu.VMEM((nodes, slots), F32),
             dma((2,)),
             dma((n,)), dma((n,)),
-            dma((2, n)), dma((2, n)),
+            dma((2, 2 * b)), dma((2, 2 * b)),
             dma((n,)), dma((n,)),
             dma((b, n)), dma((b, n)),
             dma((n,)), dma((n,)),

time: 60.1 us -> 57.4 us (0.955)
  Pallas kernels: 59.3 us -> 56.6 us
    pallas_call x1, Pallas kernels: 57.1 us -> 54.4 us  [per_device(): pl.pallas_call(functools.partial(kernel, n, nd, wscale), out_shape=(jax.S...]
where the time goes in v4:
time: 57.4 us; the launch traced here: 57.2 us
  Pallas kernels  56.6 us (99%)
  between operations  0.64 us (1%)
    pallas_call x1, Pallas kernels, per_device(): pl.pallas_call(functools.partial(kernel, n, nd, wscale), out_shape=(jax.S...  54.4 us
    pallas_call x1, Pallas kernels, per_device(): pl.pallas_call(write_out, out_shape=(jax.ShapeDtypeStruct((grid_dev, widt...  2.18 us

profile of v4, /device:TPU:0, one launch (start us, length us, event | category | flops | bytes accessed | tf_op | source)
XLA Modules:
  0.0 57.2 jit_solution(9530309579816595815)
XLA Ops:
  0.6 54.4 %graph_attention_grads.1 = (bf16[128,1024]{1,0:T(8,128)(2,1)}, bf16[64,1024]{1,0:T(8,128)(2,1)}, bf16[64,1024]{1,0:T(8,128)(2,1)}, bf16[64,2048]{1,0:T(8,128)(2,1)}) custom-call(bf16[128,1024]{1,0:T(8,128)(2,1)} %bitcast.7, bf16[64,1024]{1,0:T(8,128)(2,1)} %bitcast.9, bf16[128,1024]{1,0:T(8,128)(2,1)} %bitcast.8, bf16[1024,1024]{1,0:T(8,128)(2,1)} %wq_h.1, ...), custom_call_target="tpu_custom_call" | custom-call | tf_op jit(solution)/shard_map/graph_attention_grads/pallas_call | solution.py:390
  55.1 2.2 %write_out.1 = (bf16[128,1024]{1,0:T(8,128)(2,1)}, bf16[64,1024]{1,0:T(8,128)(2,1)}, f32[64,1024]{1,0:T(8,128)}, f32[64,2048]{1,0:T(8,128)}) custom-call(bf16[128,1024]{1,0:T(8,128)(2,1)} %get-tuple-element.12.d_grid, bf16[64,1024]{1,0:T(8,128)(2,1)} %get-tuple-element.13.d_nodes, bf16[64,1024]{1,0:T(8,128)(2,1)} %get-tuple-element.14.dw_query, ...), custom_call_target="tpu_custom_call" | custom-call | tf_op jit(solution)/shard_map/write_out/pallas_call | solution.py:443
